TPU v7x, 256 devices: a whole 4x4x8 slice. The times are simulated.
256 devices in a mesh: seq: 32 (over x, y, core), head: 8 (over z).
Axes of the slice: x: 4, y: 4, z: 8, core: 2. Of those that a mesh axis runs over, the one named last changes fastest.
Arguments:
- tokens: bfloat16 [32768, 2048], P('seq'), may hold values from -6 to 6
- norm_gain: bfloat16 [2048], replicated, may hold values from 0.099609375 to 1.8984375
- w_qkv: bfloat16 [3, 2048, 2048], P(None, None, 'head'), may hold values from -0.176776695 to 0.176776695
- mem_gate: float32 [16], P('head'), may hold values from -3 to 3
- w_out: bfloat16 [2048, 2048], P('head'), may hold values from -0.1875 to 0.1875
Outputs:
- attended: bfloat16 [32768, 2048], P('seq', 'head')
- memory_state: float32 [32, 16, 128, 128], P('seq', 'head')
All inputs are finite; a program needn't handle non-finite values.
Results may differ from a plain program's by a relative error of at most 0.01.
The roundings to bfloat16 on the way count: a program that leaves them out, or rounds other values in their place, can miss the bound.
Values may be sent and summed in bfloat16 or wider, within the bound.
A program may use at most 64 MiB of HBM per device.

v0:
```python
import jax
import jax.numpy as jnp
from jax import lax
from jax.sharding import PartitionSpec as P

HDIM = 128


def sent_together(arrays, axis, dim, along):
    columns = [a.reshape(*a.shape[:along], -1) for a in arrays]
    both = jnp.concatenate(columns, axis=along)
    result, at, gathered = (lax.all_gather(both, axis, axis=dim, tiled=True), 0, [])
    for a, column in zip(arrays, columns):
        section = result[..., at : at + column.shape[along]]
        gathered.append(section.reshape(*section.shape[:along], *a.shape[along:]))
        at += column.shape[along]
    return tuple(gathered)


def elu_one(values_in):
    return jnp.where(values_in > 0, values_in + 1.0, jnp.exp(jnp.minimum(values_in, 0.0)))


def on_device(tokens, norm_gain, w_qkv, mem_gate, w_out):
    seg_len = tokens.shape[0]
    local_heads = w_qkv.shape[2] // HDIM
    float_tokens = tokens.astype(jnp.float32)
    normed = (
        float_tokens
        * lax.rsqrt(jnp.mean(float_tokens * float_tokens, axis=-1, keepdims=True) + 1e-05)
        * norm_gain.astype(jnp.float32)
    ).astype(jnp.bfloat16)
    projected = jnp.einsum("td,cdh->cth", normed, w_qkv, preferred_element_type=jnp.float32).astype(
        jnp.bfloat16
    )
    queries = projected[0].reshape(seg_len, local_heads, HDIM)
    key_rows = projected[1].reshape(seg_len, local_heads, HDIM)
    value_rows = projected[2].reshape(seg_len, local_heads, HDIM)
    sig_keys = elu_one(key_rows.astype(jnp.float32))
    memory_delta = jnp.einsum("thd,the->hde", sig_keys, value_rows.astype(jnp.float32))
    delta_norm = jnp.sum(sig_keys, axis=0)
    zero_memory = jnp.zeros_like(memory_delta)
    zero_norm = jnp.zeros_like(delta_norm)
    my_index = lax.axis_index("seq")
    pieces = tuple(
        (
            part.astype(jnp.float32)
            for part in sent_together(
                (memory_delta[None].astype(jnp.bfloat16), delta_norm[None].astype(jnp.bfloat16)),
                "seq",
                0,
                3,
            )
        )
    )
    row_count = pieces[0].shape[0]
    keep_rows = (jnp.arange(row_count, dtype=jnp.int32) < my_index).astype(jnp.float32)
    memory_prev = zero_memory + jnp.sum(pieces[0] * keep_rows[:, None, None, None], axis=0)
    norm_prev = zero_norm + jnp.sum(pieces[1] * keep_rows[:, None, None], axis=0)
    inv_sqrt = 1.0 / HDIM**0.5
    scores = (
        jnp.einsum("qhd,khd->hqk", queries, key_rows, preferred_element_type=jnp.float32) * inv_sqrt
    )
    row_ids = lax.broadcasted_iota(jnp.int32, (seg_len, seg_len), 0)
    col_ids = lax.broadcasted_iota(jnp.int32, (seg_len, seg_len), 1)
    scores = jnp.where((col_ids <= row_ids)[None], scores, -1e30)
    weights = jax.nn.softmax(scores, axis=-1).astype(jnp.bfloat16)
    local_out = jnp.einsum("hqk,khd->qhd", weights, value_rows, preferred_element_type=jnp.float32)
    sig_q = elu_one(queries.astype(jnp.float32))
    retrieved = jnp.einsum("thd,hde->the", sig_q, memory_prev)
    normalizer = 1.0 + jnp.einsum("thd,hd->th", sig_q, norm_prev)
    gate_share = jax.nn.sigmoid(mem_gate)[None, :, None]
    mixed_out = (
        gate_share * retrieved / normalizer[..., None] + (1.0 - gate_share) * local_out
    ).astype(jnp.bfloat16)
    mixed_out = mixed_out.reshape(seg_len, local_heads * HDIM)
    weight_cols = lax.all_to_all(w_out, "head", split_axis=1, concat_axis=0, tiled=True)
    attended = jnp.dot(
        lax.all_gather(mixed_out, "head", axis=1, tiled=True),
        weight_cols,
        preferred_element_type=jnp.float32,
    ).astype(jnp.bfloat16)
    memory_state = ((memory_prev + memory_delta) / seg_len)[None]
    return (attended, memory_state)


def solution(mesh):
    placed = (P("seq", None), P(), P(None, None, "head"), P("head"), P("head", None))
    return jax.shard_map(
        on_device,
        mesh=mesh,
        in_specs=placed,
        out_specs=(P("seq", "head"), P("seq", "head", None, None)),
        check_vma=False,
    )
```

profile of v0, /device:TPU:32, one launch (start us, length us, event | category | flops | bytes accessed | tf_op | source)
XLA Modules:
  0.0 167.8 jit_solution(17933472047963940664)
XLA Ops:
  7.2 0.0 copy-start
  7.2 0.0 copy-start.2
  7.2 0.0 all-gather.3.cloned.1.call-start
  7.2 0.0 copy-start.1
  7.2 3.2 %fusion.1 = f32[1024]{0:T(1024)S(1)} fusion(bf16[1024,2048]{1,0:T(8,128)(2,1)} %param.5), kind=kLoop, calls=%fused_computation.3 | loop fusion | flops 6290432 | bytes 4198400 | tf_op jit(solution)/shard_map/reduce_sum | solution.py:30
  10.5 0.0 copy-done.2
  10.5 0.0 copy-done
  10.5 1.1 copy-done.1
  11.6 3.9 %fusion.17 = bf16[3,1024,256]{1,2,0:T(8,128)(2,1)S(1)} fusion(bf16[3,2048,256]{2,1,0:T(8,128)(2,1)S(1)} %copy-done, bf16[1024,2048]{1,0:T(8,128)(2,1)S(1)} %copy-done.1, f32[2048]{0:T(1024)S(1)} %convert_element_type.76, f32[1024]{0:T(1024)S(1)} %add_rsqrt_fusion), kind=kOutput, calls=%fused_computation.30 | convolution fusion | flops 3230400512 | bytes 8925184 | tf_op jit(solution)/shard_map/td,cdh->cth/dot_general | solution.py:33
  15.5 0.0 copy-start.3
  15.5 1.2 fusion.58
  16.7 0.4 fusion.32
  17.0 2.1 %copy.44 = bf16[1024,2,128]{2,0,1:T(8,128)(2,1)} copy(bf16[1024,2,128]{0,2,1:T(8,128)(2,1)} %bitcast.59) | data formatting | bytes 1048576 | tf_op jit(solution)/shard_map/reshape;squeeze | solution.py:37
  19.1 1.6 fusion.27
  20.8 0.7 copy.46
  21.4 0.0 all-gather.3.cloned.1.call-update
  21.5 0.2 all-gather.5.cloned.1.call-start
  21.7 2.1 %copy.47 = bf16[1024,2,128]{2,0,1:T(8,128)(2,1)} copy(bf16[1024,2,128]{0,2,1:T(8,128)(2,1)} %bitcast.61) | data formatting | bytes 1048576 | tf_op jit(solution)/shard_map/reshape;squeeze | solution.py:36
  23.8 1.3 iota_compare_fusion
  25.0 0.0 copy-done.3
  25.1 8.2 %fusion.59 = (f32[2,1024]{1,0:T(2,128)S(1)}, f32[2,1024,1024]{1,2,0:T(8,128)}) fusion(pred[1024,1024]{0,1:T(8,128)(4,1)} %iota_compare_fusion, bf16[1024,2,128]{0,2,1:T(8,128)(2,1)} %bitcast.62, bf16[1024,2,128]{0,2,1:T(8,128)(2,1)} %bitcast.60), kind=kOutput, calls=%fused_computation.78 | convolution fusion | flops 545260544 | bytes 10493952 | tf_op jit(solution)/shard_map/sub | solution.py:67
  33.2 5.3 %fusion.24 = f32[1024,2,128]{0,2,1:T(8,128)} fusion(bf16[1024,2,128]{0,2,1:T(8,128)(2,1)} %bitcast.66, f32[2,1024,1024]{1,2,0:T(8,128)} %get-tuple-element.18, f32[2,1024]{1,0:T(2,128)S(1)} %get-tuple-element.17, f32[2]{0:T(128)S(1)} %get-tuple-element.12), kind=kOutput, calls=%fused_computation.36 | convolution fusion | flops 541327360 | bytes 9969672 | tf_op jit(solution)/shard_map/hqk,khd->qhd/dot_general | solution.py:68
  38.5 34.6 %all-gather.3.cloned.1.call-done = bf16[32,2,128,129]{2,1,3,0:T(2,128)(2,1)} async-done(((bf16[1,2,128,129]{2,1,3,0:T(2,128)(2,1)}), bf16[32,2,128,129]{2,1,3,0:T(2,128)(2,1)}) %all-gather.3.cloned.1.call-update) | async-done | bytes 2113552 | tf_op jit(solution)/shard_map/all_gather | solution.py:12
  73.1 0.8 fusion.48
  74.0 1.4 fusion.36
  75.4 3.9 %multiply_reduce_fusion = f32[2,128,128]{1,0,2:T(2,128)S(1)} fusion(f32[32]{0:T(128)S(1)} %compare_convert_fusion, bf16[32,2,128,129]{2,1,3,0:T(2,128)(2,1)} %all-gather.3.cloned.1.call-done), kind=kLoop, calls=%fused_computation.15 | loop fusion | flops 3112960 | bytes 2228352 | tf_op jit(solution)/shard_map/reduce_sum | solution.py:58
  79.3 2.6 %fusion.25 = bf16[1024,2,128]{0,2,1:T(8,128)(2,1)} fusion(f32[1024,2,128]{0,2,1:T(8,128)} %fusion.24, bf16[1024,2,128]{2,0,1:T(8,128)(2,1)} %copy.47, f32[1024,2]{0,1:T(2,128)S(1)} %fusion.49, f32[2]{0:T(128)S(1)} %get-tuple-element.13, f32[2,128,128]{1,0,2:T(2,128)S(1)} %multiply_reduce_fusion), kind=kOutput, calls=%fused_computation.37 | convolution fusion | flops 69468160 | bytes 2236424 | tf_op jit(solution)/shard_map/thd,hde->the/dot_general | solution.py:70
  82.0 0.0 all-gather.5.cloned.1.call-update
  82.0 2.3 %copy.52 = bf16[256,2048]{0,1:T(8,128)(2,1)} copy(bf16[256,2048]{1,0:T(8,128)(2,1)} %param.9) | data formatting | bytes 2097152 | tf_op args[4]
  84.3 46.5 %all_to_all.19 = bf16[256,8,256]{0,2,1:T(8,128)(2,1)} all-to-all(bf16[256,8,256]{0,2,1:T(8,128)(2,1)} %bitcast.58), channel_id=1, replica_groups=mesh['seq'=32,'head'=8] {'head'}, dimensions={1} | all-to-all | bytes 2097152 | tf_op jit(solution)/shard_map/all_to_all | solution.py:77
  130.8 2.3 %copy.53 = bf16[8,256,256]{2,1,0:T(8,128)(2,1)} copy(bf16[8,256,256]{1,2,0:T(8,128)(2,1)} %bitcast.57) | data formatting | bytes 2097152 | tf_op jit(solution)/shard_map/all_to_all | solution.py:77
  133.1 0.8 copy.55
  133.9 22.5 %all-gather.5.cloned.1.call-done = bf16[1024,2048]{0,1:T(8,128)(2,1)} async-done(((bf16[1024,256]{0,1:T(8,128)(2,1)}), bf16[1024,2048]{0,1:T(8,128)(2,1)}) %all-gather.5.cloned.1.call-update) | async-done | bytes 4194320 | tf_op jit(solution)/shard_map/all_gather | solution.py:79
  156.4 4.6 %convolution_convert_fusion = bf16[1024,256]{1,0:T(8,128)(2,1)} fusion(bf16[1024,2048]{0,1:T(8,128)(2,1)} %all-gather.5.cloned.1.call-done, bf16[2048,256]{1,0:T(8,128)(2,1)} %bitcast.63), kind=kOutput, calls=%fused_computation.38 | convolution fusion | flops 1074003968 | bytes 5767168 | tf_op jit(solution)/shard_map/dot_general | solution.py:78
  (9 shorter events, 0.1 us)
Async XLA Ops:
  7.2 3.3 %copy-start = (bf16[3,2048,256]{2,1,0:T(8,128)(2,1)S(1)}, bf16[3,2048,256]{2,1,0:T(8,128)(2,1)}, u32[]{:S(2)}) copy-start(bf16[3,2048,256]{2,1,0:T(8,128)(2,1)} %param.7) | copy-start | bytes 9437188
  7.2 3.3 %copy-start.2 = (bf16[2048]{0:T(1024)(128)(2,1)S(1)}, bf16[2048]{0:T(1024)(128)(2,1)}, u32[]{:S(2)}) copy-start(bf16[2048]{0:T(1024)(128)(2,1)} %param.6) | copy-start | bytes 12292
  7.2 65.9 %all-gather.3.cloned.1.call-start = ((), (), s32[]{:S(2)}) async-start(), calls=%async_computation.1 | async-start | bytes 2179584 | tf_op jit(solution)/shard_map/all_gather | solution.py:12
  7.2 4.4 %copy-start.1 = (bf16[1024,2048]{1,0:T(8,128)(2,1)S(1)}, bf16[1024,2048]{1,0:T(8,128)(2,1)}, u32[]{:S(2)}) copy-start(bf16[1024,2048]{1,0:T(8,128)(2,1)} %param.5) | copy-start | bytes 12582916
  15.5 9.6 %copy-start.3 = (f32[2]{0:T(128)S(1)}, f32[2]{0:T(128)}, u32[]{:S(2)}) copy-start(f32[2]{0:T(128)} %param.8) | copy-start | bytes 28
  21.5 134.9 %all-gather.5.cloned.1.call-start = ((), (), s32[]{:S(2)}) async-start(), calls=%async_computation.2 | async-start | bytes 4718592 | tf_op jit(solution)/shard_map/all_gather | solution.py:79
Sparse Core Ops, SparseCore 0:
  21.6 51.5 all-gather.2
  82.1 74.1 all-gather.4
where the time goes:
time: 171 us; the launch traced here: 168 us
  waiting for transfers between devices  57.2 us (33%)
  blocking collectives  46.5 us (27%)
  matrix products  27.6 us (16%)
  between operations  14.2 us (8%)
  local copies, waits for them, and re-layouts  12.4 us (7%)
  other arithmetic  9.68 us (6%)
    all_to_all x1, blocking collectives, on_device(): lax.all_to_all(w_out, 'head', split_axis=1, concat_axis=0, tiled=True)  46.5 us
    all_gather x1, waiting for transfers between devices, sent_together(): lax.all_gather(both, axis, axis=dim, tiled=True)  34.6 us
    all_gather x1, waiting for transfers between devices, on_device(): lax.all_gather(mixed_out, 'head', axis=1, tiled=True)  22.5 us
    sub x1, matrix products, on_device(): weights = jax.nn.softmax(scores, axis=-1).astype(jnp.bfloat16)  8.15 us
    dot_general x1, matrix products, on_device(): jnp.einsum('hqk,khd->qhd', weights, value_rows, preferred_element_type=jn...  5.32 us
    dot_general x1, matrix products, on_device(): jnp.dot(lax.all_gather(mixed_out, 'head', axis=1, tiled=True), weight_col...  4.58 us
    unnamed x10, local copies, waits for them, and re-layouts  4.15 us
    reduce_sum x1, other arithmetic, on_device(): jnp.sum(pieces[0] * keep_rows[:, None, None, None], axis=0)  3.93 us
  transfers between devices with their start and end apart: 2, of which 2 were waited for; matrix products, arithmetic and copies ran while one was open for 13% of the time, Pallas kernels for 0%

commit v1 on v0

v1 whole, which is shorter than its diff:
```python
import functools

import jax
import jax.numpy as jnp
from jax import lax
from jax.experimental import pallas as pl
from jax.experimental.pallas import tpu as pltpu
from jax.sharding import PartitionSpec as P

HDIM = 128
MESH = pl.DeviceIdType.MESH
F32, BF16 = jnp.float32, jnp.bfloat16
ROWS = 256
LOG2E = 1.4426950408889634


def elu_one(t):
    return jnp.where(t > 0, t + 1.0, jnp.exp(jnp.minimum(t, 0.0)))


def front_kernel(
    tokens, gain, w_qkv, gate, mixed_out, state_out,
    tok, wts, qs, ks, vs, local, own, pay, got_c, got_x, got_y,
    in_sem, send_sem, recv_sem,
):
    seg = tok.shape[0]
    n_chunks = seg // ROWS
    heads = qs.shape[1] // HDIM
    s = lax.axis_index("seq")
    z = lax.axis_index("head")
    x, y, c = s // 8, lax.rem(s // 2, 4), lax.rem(s, 2)

    def at(x2, y2, c2):
        return (x2 * 8 + y2 * 2 + c2, z)

    partner = at(x, y, 1 - c)
    xs = [at(lax.rem(x + k, 4), y, c) for k in (1, 2, 3)]
    ys = [at(x, lax.rem(y + k, 4), c) for k in (1, 2, 3)]

    barrier = pltpu.get_barrier_semaphore()
    for peer in [partner] + xs + ys:
        pl.semaphore_signal(barrier, inc=1, device_id=peer, device_id_type=MESH)

    def load(i, src, dst):
        copy = pltpu.make_async_copy(src, dst, in_sem.at[i])
        copy.start()
        return copy

    rows = [pl.ds(i * ROWS, ROWS) for i in range(n_chunks)]
    tok_copies = [load(0, tokens.at[rows[0]], tok.at[rows[0]])]
    w_copies = [load(n_chunks + j, w_qkv.at[j], wts.at[j]) for j in (1, 2, 0)]
    tok_copies += [load(i, tokens.at[rows[i]], tok.at[rows[i]]) for i in range(1, n_chunks)]

    g = gain[...].astype(F32)
    for i in range(n_chunks):
        tok_copies[i].wait()
        t = tok[rows[i], :].astype(F32)
        scale = lax.rsqrt(jnp.mean(t * t, axis=-1, keepdims=True) + 1e-05)
        normed = (t * scale * g).astype(BF16)
        if i == 0:
            for copy in w_copies:
                copy.wait()
        for j, dst in ((1, ks), (2, vs), (0, qs)):
            dst[rows[i], :] = jnp.dot(normed, wts[j], preferred_element_type=F32).astype(BF16)

    norms = []
    for h in range(heads):
        cols = slice(h * HDIM, (h + 1) * HDIM)
        sig_k = elu_one(ks[:, cols].astype(F32))
        own[cols, :] = lax.dot_general(
            sig_k.astype(BF16), vs[:, cols], (((0,), (0,)), ((), ())), preferred_element_type=F32
        )
        norms.append(jnp.sum(sig_k, axis=0, keepdims=True))
    nrow = lax.broadcasted_iota(jnp.int32, (16, HDIM), 0)
    tail = jnp.zeros((16, HDIM), F32)
    for h in range(heads):
        tail = jnp.where(nrow == h, norms[h], tail)
    own[heads * HDIM :, :] = tail
    pay[0] = own[...].astype(BF16)

    def remote(i, src, dst, peer):
        copy = pltpu.make_async_remote_copy(
            src_ref=src, dst_ref=dst, send_sem=send_sem.at[i], recv_sem=recv_sem.at[i],
            device_id=peer, device_id_type=MESH,
        )
        copy.start()
        return copy

    pl.semaphore_wait(barrier, 7)
    swap = remote(0, pay.at[0], got_c, partner)

    inv_sqrt = LOG2E / HDIM**0.5
    row_ids = lax.broadcasted_iota(jnp.int32, (ROWS, ROWS), 0)
    col_ids = lax.broadcasted_iota(jnp.int32, (ROWS, ROWS), 1)
    causal = col_ids <= row_ids
    shares = jax.nn.sigmoid(gate[...])

    def attend(h, i):
        cols = slice(h * HDIM, (h + 1) * HDIM)
        end = (i + 1) * ROWS
        q = qs[rows[i], cols]
        sc = lax.dot_general(
            q, ks[:end, cols], (((1,), (1,)), ((), ())), preferred_element_type=F32
        )
        diag = jnp.where(causal, sc[:, end - ROWS :], -1e30)
        sc = diag if i == 0 else jnp.concatenate([sc[:, : end - ROWS], diag], axis=1)
        top = jnp.max(sc, axis=-1, keepdims=True)
        e = jnp.exp2((sc - top) * inv_sqrt)
        w = (e * (1.0 / jnp.sum(e, axis=-1, keepdims=True))).astype(BF16)
        out = jnp.dot(w, vs[:end, cols], preferred_element_type=F32)
        local[rows[i], cols] = (1.0 - shares[:, h : h + 1]) * out

    work = [(h, i) for h in range(heads) for i in range(n_chunks)]
    for h, i in work[:1]:
        attend(h, i)
    swap.wait()
    total = own[...] + got_c[...].astype(F32)
    pay[1] = total.astype(BF16)
    x_copies = [remote(k, pay.at[1], got_x.at[k - 1], xs[k - 1]) for k in (1, 2, 3)]
    for h, i in work[1:4]:
        attend(h, i)
    for copy in x_copies:
        copy.wait()
    before = jnp.zeros_like(total)
    for k in (1, 2, 3):
        before += jnp.where(x >= k, got_x[k - 1].astype(F32), 0.0)
    pay[2] = before.astype(BF16)
    pay[3] = (before + total).astype(BF16)
    y_copies = [
        remote(3 + k, pay.at[2 + jnp.where(y + k < 4, 1, 0)], got_y.at[k - 1], ys[k - 1])
        for k in (1, 2, 3)
    ]
    for h, i in work[4:]:
        attend(h, i)
    for copy in y_copies:
        copy.wait()
    prev = before + jnp.where(c == 1, got_c[...].astype(F32), 0.0)
    for k in (1, 2, 3):
        prev += got_y[k - 1].astype(F32)

    for h in range(heads):
        cols = slice(h * HDIM, (h + 1) * HDIM)
        state_out[0, h] = (prev[cols] + own[cols, :]) * (1.0 / seg)
        norm = prev[heads * HDIM + h : heads * HDIM + h + 1]
        norm_cols = jnp.transpose(jnp.broadcast_to(norm, (HDIM, HDIM)))
        memory = jnp.concatenate([prev[cols], norm_cols], axis=1).astype(BF16)
        share = shares[:, h : h + 1]
        for i in range(n_chunks):
            sig_q = elu_one(qs[rows[i], cols].astype(F32)).astype(BF16)
            both = jnp.dot(sig_q, memory, preferred_element_type=F32)
            got = share * both[:, :HDIM] / (1.0 + both[:, HDIM:])
            mixed_out[rows[i], cols] = (got + local[rows[i], cols]).astype(BF16)


def front(tokens, gain, w_qkv, gate):
    seg, d = tokens.shape
    width = w_qkv.shape[2]
    heads = width // HDIM
    n_chunks = seg // ROWS
    pay = (heads * HDIM + 16, HDIM)
    vmem = pl.BlockSpec(memory_space=pltpu.VMEM)
    hbm = pl.BlockSpec(memory_space=pl.ANY)
    return pl.pallas_call(
        front_kernel,
        out_shape=(
            jax.ShapeDtypeStruct((seg, width), BF16),
            jax.ShapeDtypeStruct((1, heads, HDIM, HDIM), F32),
        ),
        in_specs=[hbm, vmem, hbm, vmem],
        out_specs=(vmem, vmem),
        scratch_shapes=[
            pltpu.VMEM((seg, d), BF16),
            pltpu.VMEM((3, d, width), BF16),
            pltpu.VMEM((seg, width), BF16),
            pltpu.VMEM((seg, width), BF16),
            pltpu.VMEM((seg, width), BF16),
            pltpu.VMEM((seg, width), F32),
            pltpu.VMEM(pay, F32),
            pltpu.VMEM((4,) + pay, BF16),
            pltpu.VMEM(pay, BF16),
            pltpu.VMEM((3,) + pay, BF16),
            pltpu.VMEM((3,) + pay, BF16),
            pltpu.SemaphoreType.DMA((n_chunks + 3,)),
            pltpu.SemaphoreType.DMA((7,)),
            pltpu.SemaphoreType.DMA((7,)),
        ],
        compiler_params=pltpu.CompilerParams(
            collective_id=0, has_side_effects=True, vmem_limit_bytes=48 << 20
        ),
        name="front",
    )(tokens, gain, w_qkv, gate)


def on_device(tokens, norm_gain, w_qkv, mem_gate, w_out):
    mixed, state = front(tokens, norm_gain[None], w_qkv, mem_gate[None])
    weight_cols = lax.all_to_all(w_out, "head", split_axis=1, concat_axis=0, tiled=True)
    attended = jnp.dot(
        lax.all_gather(mixed, "head", axis=1, tiled=True),
        weight_cols,
        preferred_element_type=F32,
    ).astype(BF16)
    return attended, state


def solution(mesh):
    placed = (P("seq", None), P(), P(None, None, "head"), P("head"), P("head", None))
    return jax.shard_map(
        on_device,
        mesh=mesh,
        in_specs=placed,
        out_specs=(P("seq", "head"), P("seq", "head", None, None)),
        check_vma=False,
    )
```

time: 171 us -> 129 us (0.75); the launches traced: 168 us -> 129 us
  blocking collectives: 46.5 us -> 0 us
  Pallas kernels: 0 us -> 24.2 us
  matrix products: 27.6 us -> 4.23 us
  waiting for transfers between devices: 57.2 us -> 72.1 us
  other arithmetic: 9.68 us -> 0 us
  starting transfers between devices: 0.26 us -> 8.61 us
  local copies, waits for them, and re-layouts: 12.4 us -> 5.72 us
    all_to_all x1 -> x0, blocking collectives: 46.5 us -> none  [on_device(): lax.all_to_all(w_out, 'head', split_axis=1, concat_axis=0, tiled=True)]
    all_to_all x0 -> x1, waiting for transfers between devices: none -> 35.8 us  [on_device(): lax.all_to_all(w_out, 'head', split_axis=1, concat_axis=0, tiled=True)]
    pallas_call x0 -> x1, Pallas kernels: none -> 24.2 us  [front(): pl.pallas_call(front_kernel, out_shape=(jax.ShapeDtypeStruct((seg, width)...]
    all_gather x2 -> x1, waiting for transfers between devices: 57.1 us -> 36.3 us  [on_device(): lax.all_gather(mixed, 'head', axis=1, tiled=True)]
    dot_general x6 -> x1, matrix products: 19.5 us -> 4.23 us  [on_device(): jnp.dot(lax.all_gather(mixed, 'head', axis=1, tiled=True), weight_cols, p...]
    all_to_all x0 -> x1, starting transfers between devices: none -> 8.57 us  [on_device(): lax.all_to_all(w_out, 'head', split_axis=1, concat_axis=0, tiled=True)]
    reduce_sum x4 -> x0, other arithmetic: 8.33 us -> none  [the longest x1 3.93 us: on_device(): jnp.sum(pieces[0] * keep_rows[:, None, None, None], axis=0)]
    sub x1 -> x0, matrix products: 8.15 us -> none  [on_device(): weights = jax.nn.softmax(scores, axis=-1).astype(jnp.bfloat16)]
  transfers between devices with their start and end apart: 2 -> 2, of which waited for: 2 -> 2; matrix products, arithmetic and copies ran while one was open for 13% -> 1% of each run, Pallas kernels for 0% -> 0%
where the time goes in v1:
time: 129 us
  waiting for transfers between devices  72.1 us (56%)
  Pallas kernels  24.2 us (19%)
  between operations  14.1 us (11%)
  starting transfers between devices  8.61 us (7%)
  local copies, waits for them, and re-layouts  5.72 us (4%)
  matrix products  4.23 us (3%)
    all_gather x1, waiting for transfers between devices, on_device(): lax.all_gather(mixed, 'head', axis=1, tiled=True)  36.3 us
    all_to_all x1, waiting for transfers between devices, on_device(): lax.all_to_all(w_out, 'head', split_axis=1, concat_axis=0, tiled=True)  35.8 us
    pallas_call x1, Pallas kernels, front(): pl.pallas_call(front_kernel, out_shape=(jax.ShapeDtypeStruct((seg, width)...  24.2 us
    all_to_all x1, starting transfers between devices, on_device(): lax.all_to_all(w_out, 'head', split_axis=1, concat_axis=0, tiled=True)  8.57 us
    unnamed x8, local copies, waits for them, and re-layouts  4.51 us
    dot_general x1, matrix products, on_device(): jnp.dot(lax.all_gather(mixed, 'head', axis=1, tiled=True), weight_cols, p...  4.23 us
  transfers between devices with their start and end apart: 2, of which 2 were waited for; matrix products, arithmetic and copies ran while one was open for 1% of the time, Pallas kernels for 0%

profile of v1, /device:TPU:32, one launch (start us, length us, event | category | flops | bytes accessed | tf_op | source)
XLA Modules:
  0.0 128.9 jit_solution(4823038743648083761)
XLA Ops:
  7.2 0.0 all-gather.2.cloned.1.call-start
  7.2 0.7 broadcast_in_dim.6.gain
  7.9 0.0 copy-start
  7.9 1.9 %copy-done = bf16[3,2048,256]{2,1,0:T(8,128)(2,1)S(1)} copy-done((bf16[3,2048,256]{2,1,0:T(8,128)(2,1)S(1)}, bf16[3,2048,256]{2,1,0:T(8,128)(2,1)}, u32[]{:S(2)}) %copy-start) | copy-done | bytes 3145752
  9.8 0.0 copy-start.1
  9.8 0.7 copy-done.1
  10.4 0.0 copy-start.2
  10.5 24.2 %front.1 = (bf16[1024,256]{1,0:T(8,128)(2,1)}, f32[1,2,128,128]{3,2,1,0:T(8,128)S(1)}) custom-call(bf16[1024,2048]{1,0:T(8,128)(2,1)} %tokens.1, bf16[1,2048]{1,0:T(2,128)(2,1)S(1)} %broadcast_in_dim.6.gain, bf16[3,2048,256]{2,1,0:T(8,128)(2,1)S(1)} %copy-done, f32[1,2]{1,0:T(1,128)S(1)} %bitcast.6), custom_call_target="tpu_custom_call" | custom-call | tf_op jit(solution)/shard_map/front/pallas_call | solution.py:163
  34.7 0.0 all-gather.2.cloned.1.call-update
  34.7 0.0 copy-done.2
  34.7 1.3 %copy.7 = bf16[256,2048]{0,1:T(8,128)(2,1)} copy(bf16[256,2048]{1,0:T(8,128)(2,1)S(1)} %copy-done.2) | data formatting | bytes 2097152 | tf_op args[4]
  36.0 8.6 %all-to-all-start = ((bf16[256,8,256]{0,2,1:T(8,128)(2,1)}), bf16[256,8,256]{0,2,1:T(8,128)(2,1)S(1)}, u32[]{:S(2)}, u32[]{:S(2)}) async-start(bf16[256,8,256]{0,2,1:T(8,128)(2,1)} %bitcast.1), calls=%async_computation | async-start | bytes 2097152 | tf_op jit(solution)/shard_map/all_to_all | solution.py:196
  44.6 35.8 %all-to-all-done = bf16[256,8,256]{0,2,1:T(8,128)(2,1)S(1)} async-done(((bf16[256,8,256]{0,2,1:T(8,128)(2,1)}), bf16[256,8,256]{0,2,1:T(8,128)(2,1)S(1)}, u32[]{:S(2)}, u32[]{:S(2)}) %all-to-all-start) | async-done | bytes 1048608 | tf_op jit(solution)/shard_map/all_to_all | solution.py:196
  80.4 0.5 copy.8
  80.9 36.3 %all-gather.2.cloned.1.call-done = bf16[1024,2048]{1,0:T(8,128)(2,1)} async-done(((bf16[1024,256]{1,0:T(8,128)(2,1)}), bf16[1024,2048]{1,0:T(8,128)(2,1)}) %all-gather.2.cloned.1.call-update) | async-done | bytes 4194320 | tf_op jit(solution)/shard_map/all_gather | solution.py:198
  117.2 4.2 %convolution_convert_fusion = bf16[1024,256]{1,0:T(8,128)(2,1)} fusion(bf16[1024,2048]{1,0:T(8,128)(2,1)} %all-gather.2.cloned.1.call-done, bf16[2048,256]{1,0:T(8,128)(2,1)S(1)} %bitcast.8), kind=kOutput, calls=%fused_computation | convolution fusion | flops 1074003968 | bytes 5767168 | tf_op jit(solution)/shard_map/dot_general | solution.py:197
  121.4 0.7 copy.10
Async XLA Ops:
  7.2 110.0 %all-gather.2.cloned.1.call-start = ((), (), s32[]{:S(2)}) async-start(), calls=%async_computation.1 | async-start | bytes 4718592 | tf_op jit(solution)/shard_map/all_gather | solution.py:198
  7.9 1.9 %copy-start = (bf16[3,2048,256]{2,1,0:T(8,128)(2,1)S(1)}, bf16[3,2048,256]{2,1,0:T(8,128)(2,1)}, u32[]{:S(2)}) copy-start(bf16[3,2048,256]{2,1,0:T(8,128)(2,1)} %w_qkv.1) | copy-start | bytes 9437188
  9.8 0.7 copy-start.1
  10.4 24.3 %copy-start.2 = (bf16[256,2048]{1,0:T(8,128)(2,1)S(1)}, bf16[256,2048]{1,0:T(8,128)(2,1)}, u32[]{:S(2)}) copy-start(bf16[256,2048]{1,0:T(8,128)(2,1)} %param.9) | copy-start | bytes 3145732
  36.0 44.3 %all-to-all-start = ((bf16[256,8,256]{0,2,1:T(8,128)(2,1)}), bf16[256,8,256]{0,2,1:T(8,128)(2,1)S(1)}, u32[]{:S(2)}, u32[]{:S(2)}) async-start(bf16[256,8,256]{0,2,1:T(8,128)(2,1)} %bitcast.1), calls=%async_computation | async-start | bytes 2097152 | tf_op jit(solution)/shard_map/all_to_all | solution.py:196
Sparse Core Ops, SparseCore 0:
  34.8 82.3 all-gather.1

commit v2 on v1

v2 whole, which is shorter than its diff:
```python
import functools

import jax
import jax.numpy as jnp
from jax import lax
from jax.experimental import pallas as pl
from jax.experimental.pallas import tpu as pltpu
from jax.sharding import PartitionSpec as P

HDIM = 128
MESH = pl.DeviceIdType.MESH
F32, BF16 = jnp.float32, jnp.bfloat16
ROWS = 256
LOG2E = 1.4426950408889634


def elu_one(t):
    return jnp.where(t > 0, t + 1.0, jnp.exp(jnp.minimum(t, 0.0)))


def block_kernel(
    tokens, gain, w_qkv, gate, w_out, att_out, state_out,
    tok, wts, qs, ks, vs, local, own, pay, got_c, got_x, got_y,
    mine, mix, wown, wf, outs,
    in_sem, send_sem, recv_sem,
):
    seg = tok.shape[0]
    n_chunks = seg // ROWS
    heads = qs.shape[1] // HDIM
    width = heads * HDIM
    s = lax.axis_index("seq")
    z = lax.axis_index("head")
    x, y, c = s // 8, lax.rem(s // 2, 4), lax.rem(s, 2)
    pair = z // 2
    sign = 2 * lax.rem(z, 2) - 1

    def plane(off):
        return lax.rem(z + sign * off + 8, 8)

    def at(x2, y2, c2):
        return (x2 * 8 + y2 * 2 + c2, z)

    partner = at(x, y, 1 - c)
    xs = [at(lax.rem(x + k, 4), y, c) for k in (1, 2, 3)]
    ys = [at(x, lax.rem(y + k, 4), c) for k in (1, 2, 3)]
    zs = [(s, lax.rem(z + k, 8)) for k in range(1, 8)]
    peers = [partner] + xs + ys + zs

    barrier = pltpu.get_barrier_semaphore()
    for peer in peers:
        pl.semaphore_signal(barrier, inc=1, device_id=peer, device_id_type=MESH)

    def load(i, src, dst):
        copy = pltpu.make_async_copy(src, dst, in_sem.at[i])
        copy.start()
        return copy

    used = [0]

    def remote(src, dst, peer):
        i = used[0]
        used[0] += 1
        copy = pltpu.make_async_remote_copy(
            src_ref=src, dst_ref=dst, send_sem=send_sem.at[i], recv_sem=recv_sem.at[i],
            device_id=peer, device_id_type=MESH,
        )
        copy.start()
        return copy

    def feature_block(owner):
        return pl.ds(pl.multiple_of(owner * width, width), width)

    rows = [pl.ds(i * ROWS, ROWS) for i in range(n_chunks)]
    tok_copies = [load(0, tokens.at[rows[0]], tok.at[rows[0]])]
    w_copies = [load(n_chunks + j, w_qkv.at[j], wts.at[j]) for j in (1, 2, 0)]
    tok_copies += [load(i, tokens.at[rows[i]], tok.at[rows[i]]) for i in range(1, n_chunks)]
    own_copies = [
        load(n_chunks + 3 + k, w_out.at[:, feature_block(plane(k))], wown.at[k]) for k in range(4)
    ]

    g = gain[...].astype(F32).reshape(1, tok.shape[1])

    def project(i):
        tok_copies[i].wait()
        t = tok[rows[i], :].astype(F32)
        scale = lax.rsqrt(jnp.mean(t * t, axis=-1, keepdims=True) + 1e-05)
        normed = (t * scale * g).astype(BF16)
        if i == 0:
            for copy in w_copies:
                copy.wait()
        for j, dst in ((1, ks), (2, vs), (0, qs)):
            dst[rows[i], :] = jnp.dot(normed, wts[j], preferred_element_type=F32).astype(BF16)

    project(0)
    pl.semaphore_wait(barrier, len(peers))
    z_copies = []
    slice_rows = pl.ds(pl.multiple_of((x * 4 + y) * 16, 16), 16)
    for k in range(1, 8):
        there = lax.rem(z + k, 8)
        there_sign = 2 * lax.rem(there, 2) - 1
        for q in range(2):
            owner = lax.rem(there + there_sign * (2 * c + q) + 8, 8)
            z_copies.append(remote(
                w_out.at[slice_rows, feature_block(owner)],
                wf.at[7 - k, 2 * c + q, x, y], zs[k - 1],
            ))
    for i in range(1, n_chunks):
        project(i)

    norms = []
    for h in range(heads):
        cols = slice(h * HDIM, (h + 1) * HDIM)
        sig_k = elu_one(ks[:, cols].astype(F32))
        own[cols, :] = lax.dot_general(
            sig_k.astype(BF16), vs[:, cols], (((0,), (0,)), ((), ())), preferred_element_type=F32
        )
        norms.append(jnp.sum(sig_k, axis=0, keepdims=True))
    nrow = lax.broadcasted_iota(jnp.int32, (16, HDIM), 0)
    tail = jnp.zeros((16, HDIM), F32)
    for h in range(heads):
        tail = jnp.where(nrow == h, norms[h], tail)
    own[heads * HDIM :, :] = tail
    pay[0] = own[...].astype(BF16)
    swap = remote(pay.at[0], got_c, partner)

    inv_sqrt = LOG2E / HDIM**0.5
    row_ids = lax.broadcasted_iota(jnp.int32, (ROWS, ROWS), 0)
    col_ids = lax.broadcasted_iota(jnp.int32, (ROWS, ROWS), 1)
    causal = col_ids <= row_ids
    shares = [jax.nn.sigmoid(jnp.full((1, HDIM), gate[h], F32)) for h in range(heads)]

    def attend(h, i):
        cols = slice(h * HDIM, (h + 1) * HDIM)
        end = (i + 1) * ROWS
        q = qs[rows[i], cols]
        sc = lax.dot_general(
            q, ks[:end, cols], (((1,), (1,)), ((), ())), preferred_element_type=F32
        )
        diag = jnp.where(causal, sc[:, end - ROWS :], -1e30)
        sc = diag if i == 0 else jnp.concatenate([sc[:, : end - ROWS], diag], axis=1)
        top = jnp.max(sc, axis=-1, keepdims=True)
        e = jnp.exp2((sc - top) * inv_sqrt)
        w = (e * (1.0 / jnp.sum(e, axis=-1, keepdims=True))).astype(BF16)
        out = jnp.dot(w, vs[:end, cols], preferred_element_type=F32)
        local[rows[i], cols] = (1.0 - shares[h]) * out

    work = [(h, i) for h in range(heads) for i in range(n_chunks)]
    for copy in z_copies:
        copy.wait()
    one = [remote(wf.at[:, 2 * c, x, y], wf.at[:, 2 * c, x, y], peer) for peer in xs]
    one += [remote(wf.at[:, 2 * c + 1, x, y], wf.at[:, 2 * c + 1, x, y], peer) for peer in ys]
    for h, i in work[:1]:
        attend(h, i)
    swap.wait()
    total = own[...] + got_c[...].astype(F32)
    pay[1] = total.astype(BF16)
    x_copies = [remote(pay.at[1], got_x.at[k - 1], xs[k - 1]) for k in (1, 2, 3)]
    for h, i in work[1:4]:
        attend(h, i)
    for copy in x_copies:
        copy.wait()
    before = jnp.zeros_like(total)
    for k in (1, 2, 3):
        before += jnp.where(x >= k, got_x[k - 1].astype(F32), 0.0)
    pay[2] = before.astype(BF16)
    pay[3] = (before + total).astype(BF16)
    y_copies = [
        remote(pay.at[2 + jnp.where(y + k < 4, 1, 0)], got_y.at[k - 1], ys[k - 1])
        for k in (1, 2, 3)
    ]
    for copy in one:
        copy.wait()
    two = [remote(wf.at[:, 2 * c, :, y], wf.at[:, 2 * c, :, y], peer) for peer in ys]
    two += [remote(wf.at[:, 2 * c + 1, x], wf.at[:, 2 * c + 1, x], peer) for peer in xs]
    for h, i in work[4:]:
        attend(h, i)
    for copy in y_copies:
        copy.wait()
    prev = before + jnp.where(c == 1, got_c[...].astype(F32), 0.0)
    for k in (1, 2, 3):
        prev += got_y[k - 1].astype(F32)

    memories = []
    for h in range(heads):
        cols = slice(h * HDIM, (h + 1) * HDIM)
        state_out[0, h] = (prev[cols] + own[cols, :]) * (1.0 / seg)
        norm = prev[heads * HDIM + h : heads * HDIM + h + 1]
        norm_cols = jnp.transpose(jnp.broadcast_to(norm, (HDIM, HDIM)))
        memories.append(jnp.concatenate([prev[cols], norm_cols], axis=1).astype(BF16))

    def blend(slot, quarter):
        block = pl.ds(pl.multiple_of(quarter * ROWS, ROWS), ROWS)
        for h in range(heads):
            cols = slice(h * HDIM, (h + 1) * HDIM)
            sig_q = elu_one(qs[block, cols].astype(F32)).astype(BF16)
            both = jnp.dot(sig_q, memories[h], preferred_element_type=F32)
            got = shares[h] * both[:, :HDIM] / (1.0 + both[:, HDIM:])
            mine[slot, :, cols] = (got + local[block, cols]).astype(BF16)

    towards = {1: plane(1), 2: plane(-2), 3: plane(3)}
    straight = {}
    for k in (3, 2, 1):
        blend(k, towards[k] // 2)
        straight[k] = remote(mine.at[k], mix.at[k - 1], (s, towards[k]))
    blend(0, pair)
    beside = (s, plane(-1))
    next_door = remote(mine.at[0], mix.at[3], beside)
    handed = {}
    for k in (1, 2, 3):
        straight[k].wait()
        handed[k] = remote(mix.at[k - 1], mix.at[3 + k], beside)
    for copy in two:
        copy.wait()
    both_cores = remote(wf.at[:, pl.ds(2 * c, 2)], wf.at[:, pl.ds(2 * c, 2)], partner)
    for copy in own_copies:
        copy.wait()
    next_door.wait()
    both_cores.wait()

    def place(off):
        return lax.rem(sign * off + 8, 8) - 1

    def weight(off, k):
        return wf[place(off), k].reshape(width, width)

    sums = []
    for k in range(4):
        acc = jnp.dot(mine[0], wown[k], preferred_element_type=F32)
        for slot, off in ((0, 1), (1, 2), (2, 3), (3, -1)):
            acc += jnp.dot(mix[slot], weight(off, k), preferred_element_type=F32)
        sums.append(acc)
    for k in (1, 2, 3):
        handed[k].wait()
    here = pl.ds(pl.multiple_of(pair * ROWS, ROWS), ROWS)
    last = []
    for k in (3, 2, 1, 0):
        acc = sums[k]
        for slot, off in ((4, -2), (5, -3), (6, -4)):
            acc += jnp.dot(mix[slot], weight(off, k), preferred_element_type=F32)
        if k == 0:
            att_out[here, :] = acc.astype(BF16)
        else:
            outs[k - 1] = acc.astype(BF16)
            last.append(remote(outs.at[k - 1], att_out.at[here], (s, plane(k))))
    for copy in last:
        copy.wait()


def block(tokens, gain, w_qkv, gate, w_out):
    seg, d = tokens.shape
    width = w_qkv.shape[2]
    heads = width // HDIM
    n_chunks = seg // ROWS
    pay = (heads * HDIM + 16, HDIM)
    vmem = pl.BlockSpec(memory_space=pltpu.VMEM)
    hbm = pl.BlockSpec(memory_space=pl.ANY)
    return pl.pallas_call(
        block_kernel,
        out_shape=(
            jax.ShapeDtypeStruct((seg, width), BF16),
            jax.ShapeDtypeStruct((1, heads, HDIM, HDIM), F32),
        ),
        in_specs=[hbm, vmem, hbm, pl.BlockSpec(memory_space=pltpu.SMEM), hbm],
        out_specs=(vmem, vmem),
        scratch_shapes=[
            pltpu.VMEM((seg, d), BF16),
            pltpu.VMEM((3, d, width), BF16),
            pltpu.VMEM((seg, width), BF16),
            pltpu.VMEM((seg, width), BF16),
            pltpu.VMEM((seg, width), BF16),
            pltpu.VMEM((seg, width), F32),
            pltpu.VMEM(pay, F32),
            pltpu.VMEM((4,) + pay, BF16),
            pltpu.VMEM(pay, BF16),
            pltpu.VMEM((3,) + pay, BF16),
            pltpu.VMEM((3,) + pay, BF16),
            pltpu.VMEM((4, ROWS, width), BF16),
            pltpu.VMEM((7, ROWS, width), BF16),
            pltpu.VMEM((4, width, width), BF16),
            pltpu.VMEM((7, 4, 4, 4, 16, width), BF16),
            pltpu.VMEM((3, ROWS, width), BF16),
            pltpu.SemaphoreType.DMA((n_chunks + 7,)),
            pltpu.SemaphoreType.DMA((48,)),
            pltpu.SemaphoreType.DMA((48,)),
        ],
        compiler_params=pltpu.CompilerParams(
            collective_id=0, has_side_effects=True, vmem_limit_bytes=60 << 20
        ),
        name="block",
    )(tokens, gain, w_qkv, gate, w_out)


def settle_kernel(att, state, att_out, state_out):
    att_out[...] = att[...]
    state_out[...] = state[...]


def settle(*arrays):
    vmem = pl.BlockSpec(memory_space=pltpu.VMEM)
    return pl.pallas_call(
        settle_kernel,
        out_shape=tuple(jax.ShapeDtypeStruct(a.shape, a.dtype) for a in arrays),
        in_specs=[vmem, vmem],
        out_specs=(vmem, vmem),
        compiler_params=pltpu.CompilerParams(vmem_limit_bytes=60 << 20),
        name="settle",
    )(*arrays)


def on_device(tokens, norm_gain, w_qkv, mem_gate, w_out):
    return settle(*block(tokens, norm_gain, w_qkv, mem_gate, w_out))


def solution(mesh):
    placed = (P("seq", None), P(), P(None, None, "head"), P("head"), P("head", None))
    return jax.shard_map(
        on_device,
        mesh=mesh,
        in_specs=placed,
        out_specs=(P("seq", "head"), P("seq", "head", None, None)),
        check_vma=False,
    )
```

time: 129 us -> 64.4 us (0.50)
  waiting for transfers between devices: 72.1 us -> 0 us
  Pallas kernels: 24.2 us -> 63.7 us
  between operations: 14.1 us -> 0.64 us
  starting transfers between devices: 8.61 us -> 0 us
  local copies, waits for them, and re-layouts: 5.72 us -> 0 us
  matrix products: 4.23 us -> 0 us
    pallas_call x1 -> x2, Pallas kernels: 24.2 us -> 63.7 us  [the longest x1 61.7 us: block(): pl.pallas_call(block_kernel, out_shape=(jax.ShapeDtypeStruct((seg, width)...]
    all_gather x1 -> x0, waiting for transfers between devices: 36.3 us -> none  [on_device(): lax.all_gather(mixed, 'head', axis=1, tiled=True)]
    all_to_all x1 -> x0, waiting for transfers between devices: 35.8 us -> none  [on_device(): lax.all_to_all(w_out, 'head', split_axis=1, concat_axis=0, tiled=True)]
    all_to_all x1 -> x0, starting transfers between devices: 8.57 us -> none  [on_device(): lax.all_to_all(w_out, 'head', split_axis=1, concat_axis=0, tiled=True)]
    unnamed x8 -> x0, local copies, waits for them, and re-layouts: 4.51 us -> none
    dot_general x1 -> x0, matrix products: 4.23 us -> none  [on_device(): jnp.dot(lax.all_gather(mixed, 'head', axis=1, tiled=True), weight_cols, p...]
  transfers between devices with their start and end apart: 2 -> 0, of which waited for: 2 -> 0; matrix products, arithmetic and copies ran while one was open for 1% -> 0% of each run, Pallas kernels for 0% -> 0%
where the time goes in v2:
time: 64.4 us; the launch traced here: 64.3 us
  Pallas kernels  63.7 us (99%)
    pallas_call x1, Pallas kernels, block(): pl.pallas_call(block_kernel, out_shape=(jax.ShapeDtypeStruct((seg, width)...  61.7 us
    pallas_call x1, Pallas kernels, settle(): pl.pallas_call(settle_kernel, out_shape=tuple((jax.ShapeDtypeStruct(a.sha...  1.93 us

profile of v2, /device:TPU:32, one launch (start us, length us, event | category | flops | bytes accessed | tf_op | source)
XLA Modules:
  0.0 64.3 jit_solution(6987832087892022)
XLA Ops:
  0.6 61.7 %block.1 = (bf16[1024,256]{1,0:T(8,128)(2,1)}, f32[1,2,128,128]{3,2,1,0:T(8,128)}) custom-call(bf16[1024,2048]{1,0:T(8,128)(2,1)} %tokens.1, bf16[2048]{0:T(1024)(128)(2,1)} %gain.1, bf16[3,2048,256]{2,1,0:T(8,128)(2,1)} %w_qkv.1, f32[2]{0:T(128)} %gate.1, bf16[256,2048]{1,0:T(8,128)(2,1)} %w_out.1), custom_call_target="tpu_custom_call" | custom-call | tf_op jit(solution)/shard_map/block/pallas_call | solution.py:257
  62.4 1.9 %settle.1 = (bf16[1024,256]{1,0:T(8,128)(2,1)}, f32[1,2,128,128]{3,2,1,0:T(8,128)}) custom-call(bf16[1024,256]{1,0:T(8,128)(2,1)} %get-tuple-element.4.att, f32[1,2,128,128]{3,2,1,0:T(8,128)} %get-tuple-element.5.state), custom_call_target="tpu_custom_call" | custom-call | tf_op jit(solution)/shard_map/settle/pallas_call | solution.py:300

commit v3 on v2

--- a/solution.py
+++ b/solution.py
@@ -80,32 +80,37 @@
 
     g = gain[...].astype(F32).reshape(1, tok.shape[1])
 
-    def project(i):
+    def normalize(i):
         tok_copies[i].wait()
         t = tok[rows[i], :].astype(F32)
         scale = lax.rsqrt(jnp.mean(t * t, axis=-1, keepdims=True) + 1e-05)
-        normed = (t * scale * g).astype(BF16)
+        tok[rows[i], :] = (t * scale * g).astype(BF16)
+
+    def project(i, j, dst):
+        out = jnp.dot(tok[rows[i], :], wts[j], preferred_element_type=F32)
+        dst[rows[i], :] = out.astype(BF16)
+
+    normalize(0)
+    w_copies[0].wait()
+    w_copies[1].wait()
+    for i in range(n_chunks):
+        if i + 1 < n_chunks:
+            normalize(i + 1)
+        project(i, 1, ks)
+        project(i, 2, vs)
         if i == 0:
-            for copy in w_copies:
-                copy.wait()
-        for j, dst in ((1, ks), (2, vs), (0, qs)):
-            dst[rows[i], :] = jnp.dot(normed, wts[j], preferred_element_type=F32).astype(BF16)
-
-    project(0)
-    pl.semaphore_wait(barrier, len(peers))
-    z_copies = []
-    slice_rows = pl.ds(pl.multiple_of((x * 4 + y) * 16, 16), 16)
-    for k in range(1, 8):
-        there = lax.rem(z + k, 8)
-        there_sign = 2 * lax.rem(there, 2) - 1
-        for q in range(2):
-            owner = lax.rem(there + there_sign * (2 * c + q) + 8, 8)
-            z_copies.append(remote(
-                w_out.at[slice_rows, feature_block(owner)],
-                wf.at[7 - k, 2 * c + q, x, y], zs[k - 1],
-            ))
-    for i in range(1, n_chunks):
-        project(i)
+            pl.semaphore_wait(barrier, len(peers))
+            z_copies = []
+            slice_rows = pl.ds(pl.multiple_of((x * 4 + y) * 16, 16), 16)
+            for k in range(1, 8):
+                there = lax.rem(z + k, 8)
+                there_sign = 2 * lax.rem(there, 2) - 1
+                for q in range(2):
+                    owner = lax.rem(there + there_sign * (2 * c + q) + 8, 8)
+                    z_copies.append(remote(
+                        w_out.at[slice_rows, feature_block(owner)],
+                        wf.at[7 - k, 2 * c + q, x, y], zs[k - 1],
+                    ))
 
     norms = []
     for h in range(heads):
@@ -145,17 +150,18 @@
         local[rows[i], cols] = (1.0 - shares[h]) * out
 
     work = [(h, i) for h in range(heads) for i in range(n_chunks)]
+    w_copies[2].wait()
+    for i in range(n_chunks):
+        project(i, 0, qs)
     for copy in z_copies:
         copy.wait()
     one = [remote(wf.at[:, 2 * c, x, y], wf.at[:, 2 * c, x, y], peer) for peer in xs]
     one += [remote(wf.at[:, 2 * c + 1, x, y], wf.at[:, 2 * c + 1, x, y], peer) for peer in ys]
-    for h, i in work[:1]:
-        attend(h, i)
     swap.wait()
     total = own[...] + got_c[...].astype(F32)
     pay[1] = total.astype(BF16)
     x_copies = [remote(pay.at[1], got_x.at[k - 1], xs[k - 1]) for k in (1, 2, 3)]
-    for h, i in work[1:4]:
+    for h, i in work[:4]:
         attend(h, i)
     for copy in x_copies:
         copy.wait()
@@ -172,8 +178,14 @@
         copy.wait()
     two = [remote(wf.at[:, 2 * c, :, y], wf.at[:, 2 * c, :, y], peer) for peer in ys]
     two += [remote(wf.at[:, 2 * c + 1, x], wf.at[:, 2 * c + 1, x], peer) for peer in xs]
+    across = [
+        remote(wf.at[:, 2 * c, :, y], wf.at[:, 2 * c, :, y], partner),
+        remote(wf.at[:, 2 * c + 1, x], wf.at[:, 2 * c + 1, x], partner),
+    ]
     for h, i in work[4:]:
         attend(h, i)
+    for i in range(n_chunks):
+        qs[rows[i], :] = elu_one(qs[rows[i], :].astype(F32)).astype(BF16)
     for copy in y_copies:
         copy.wait()
     prev = before + jnp.where(c == 1, got_c[...].astype(F32), 0.0)
@@ -188,34 +200,41 @@
         norm_cols = jnp.transpose(jnp.broadcast_to(norm, (HDIM, HDIM)))
         memories.append(jnp.concatenate([prev[cols], norm_cols], axis=1).astype(BF16))
 
-    def blend(slot, quarter):
-        block = pl.ds(pl.multiple_of(quarter * ROWS, ROWS), ROWS)
+    half = ROWS // 2
+
+    def blend(slot, quarter, t):
+        block = pl.ds(pl.multiple_of(quarter * ROWS + t * half, half), half)
         for h in range(heads):
             cols = slice(h * HDIM, (h + 1) * HDIM)
-            sig_q = elu_one(qs[block, cols].astype(F32)).astype(BF16)
-            both = jnp.dot(sig_q, memories[h], preferred_element_type=F32)
+            both = jnp.dot(qs[block, cols], memories[h], preferred_element_type=F32)
             got = shares[h] * both[:, :HDIM] / (1.0 + both[:, HDIM:])
-            mine[slot, :, cols] = (got + local[block, cols]).astype(BF16)
+            mine[slot, t, :, cols] = (got + local[block, cols]).astype(BF16)
 
     towards = {1: plane(1), 2: plane(-2), 3: plane(3)}
-    straight = {}
-    for k in (3, 2, 1):
-        blend(k, towards[k] // 2)
-        straight[k] = remote(mine.at[k], mix.at[k - 1], (s, towards[k]))
-    blend(0, pair)
     beside = (s, plane(-1))
-    next_door = remote(mine.at[0], mix.at[3], beside)
-    handed = {}
-    for k in (1, 2, 3):
-        straight[k].wait()
-        handed[k] = remote(mix.at[k - 1], mix.at[3 + k], beside)
-    for copy in two:
-        copy.wait()
-    both_cores = remote(wf.at[:, pl.ds(2 * c, 2)], wf.at[:, pl.ds(2 * c, 2)], partner)
+    straight, next_door, handed = {}, {}, {}
+    for t in range(2):
+        for k in (3, 2, 1):
+            blend(k, towards[k] // 2, t)
+            straight[t, k] = remote(mine.at[k, t], mix.at[k - 1, t], (s, towards[k]))
+        blend(0, pair, t)
+        next_door[t] = remote(mine.at[0, t], mix.at[3, t], beside)
+    for t in range(2):
+        for k in (1, 2, 3):
+            straight[t, k].wait()
+            handed[t, k] = remote(mix.at[k - 1, t], mix.at[3 + k, t], beside)
+        if t == 0:
+            for k in (1, 2, 3):
+                two[k - 1].wait()
+                spot = wf.at[:, 2 * c, :, lax.rem(y + 4 - k, 4)]
+                across.append(remote(spot, spot, partner))
+                two[k + 2].wait()
+                spot = wf.at[:, 2 * c + 1, lax.rem(x + 4 - k, 4)]
+                across.append(remote(spot, spot, partner))
     for copy in own_copies:
         copy.wait()
-    next_door.wait()
-    both_cores.wait()
+    for copy in across:
+        copy.wait()
 
     def place(off):
         return lax.rem(sign * off + 8, 8) - 1
@@ -223,25 +242,27 @@
     def weight(off, k):
         return wf[place(off), k].reshape(width, width)
 
-    sums = []
-    for k in range(4):
-        acc = jnp.dot(mine[0], wown[k], preferred_element_type=F32)
-        for slot, off in ((0, 1), (1, 2), (2, 3), (3, -1)):
-            acc += jnp.dot(mix[slot], weight(off, k), preferred_element_type=F32)
-        sums.append(acc)
-    for k in (1, 2, 3):
-        handed[k].wait()
-    here = pl.ds(pl.multiple_of(pair * ROWS, ROWS), ROWS)
     last = []
-    for k in (3, 2, 1, 0):
-        acc = sums[k]
-        for slot, off in ((4, -2), (5, -3), (6, -4)):
-            acc += jnp.dot(mix[slot], weight(off, k), preferred_element_type=F32)
-        if k == 0:
-            att_out[here, :] = acc.astype(BF16)
-        else:
-            outs[k - 1] = acc.astype(BF16)
-            last.append(remote(outs.at[k - 1], att_out.at[here], (s, plane(k))))
+    for t in range(2):
+        next_door[t].wait()
+        sums = []
+        for k in range(4):
+            acc = jnp.dot(mine[0, t], wown[k], preferred_element_type=F32)
+            for slot, off in ((0, 1), (1, 2), (2, 3), (3, -1)):
+                acc += jnp.dot(mix[slot, t], weight(off, k), preferred_element_type=F32)
+            sums.append(acc)
+        for k in (1, 2, 3):
+            handed[t, k].wait()
+        here = pl.ds(pl.multiple_of(pair * ROWS + t * half, half), half)
+        for k in (3, 2, 1, 0):
+            acc = sums[k]
+            for slot, off in ((4, -2), (5, -3), (6, -4)):
+                acc += jnp.dot(mix[slot, t], weight(off, k), preferred_element_type=F32)
+            if k == 0:
+                att_out[here, :] = acc.astype(BF16)
+            else:
+                outs[k - 1, t] = acc.astype(BF16)
+                last.append(remote(outs.at[k - 1, t], att_out.at[here], (s, plane(k))))
     for copy in last:
         copy.wait()
 
@@ -274,14 +295,14 @@
             pltpu.VMEM(pay, BF16),
             pltpu.VMEM((3,) + pay, BF16),
             pltpu.VMEM((3,) + pay, BF16),
-            pltpu.VMEM((4, ROWS, width), BF16),
-            pltpu.VMEM((7, ROWS, width), BF16),
+            pltpu.VMEM((4, 2, ROWS // 2, width), BF16),
+            pltpu.VMEM((7, 2, ROWS // 2, width), BF16),
             pltpu.VMEM((4, width, width), BF16),
             pltpu.VMEM((7, 4, 4, 4, 16, width), BF16),
-            pltpu.VMEM((3, ROWS, width), BF16),
+            pltpu.VMEM((3, 2, ROWS // 2, width), BF16),
             pltpu.SemaphoreType.DMA((n_chunks + 7,)),
-            pltpu.SemaphoreType.DMA((48,)),
-            pltpu.SemaphoreType.DMA((48,)),
+            pltpu.SemaphoreType.DMA((64,)),
+            pltpu.SemaphoreType.DMA((64,)),
         ],
         compiler_params=pltpu.CompilerParams(
             collective_id=0, has_side_effects=True, vmem_limit_bytes=60 << 20

time: 64.4 us -> 59.8 us (0.929); the launches traced: 64.3 us -> 58.8 us
  Pallas kernels: 63.7 us -> 58.2 us
    pallas_call x1, Pallas kernels: 61.7 us -> 56.3 us  [block(): pl.pallas_call(block_kernel, out_shape=(jax.ShapeDtypeStruct((seg, width)...]
where the time goes in v3:
time: 59.8 us; the launch traced here: 58.8 us
  Pallas kernels  58.2 us (97%)
  between operations  0.64 us (1%)
    pallas_call x1, Pallas kernels, block(): pl.pallas_call(block_kernel, out_shape=(jax.ShapeDtypeStruct((seg, width)...  56.3 us
    pallas_call x1, Pallas kernels, settle(): pl.pallas_call(settle_kernel, out_shape=tuple((jax.ShapeDtypeStruct(a.sha...  1.93 us

profile of v3, /device:TPU:32, one launch (start us, length us, event | category | flops | bytes accessed | tf_op | source)
XLA Modules:
  0.0 58.8 jit_solution(5382643882529712610)
XLA Ops:
  0.6 56.3 %block.1 = (bf16[1024,256]{1,0:T(8,128)(2,1)}, f32[1,2,128,128]{3,2,1,0:T(8,128)}) custom-call(bf16[1024,2048]{1,0:T(8,128)(2,1)} %tokens.1, bf16[2048]{0:T(1024)(128)(2,1)} %gain.1, bf16[3,2048,256]{2,1,0:T(8,128)(2,1)} %w_qkv.1, f32[2]{0:T(128)} %gate.1, bf16[256,2048]{1,0:T(8,128)(2,1)} %w_out.1), custom_call_target="tpu_custom_call" | custom-call | tf_op jit(solution)/shard_map/block/pallas_call | solution.py:278
  56.9 1.9 %settle.1 = (bf16[1024,256]{1,0:T(8,128)(2,1)}, f32[1,2,128,128]{3,2,1,0:T(8,128)}) custom-call(bf16[1024,256]{1,0:T(8,128)(2,1)} %get-tuple-element.4.att, f32[1,2,128,128]{3,2,1,0:T(8,128)} %get-tuple-element.5.state), custom_call_target="tpu_custom_call" | custom-call | tf_op jit(solution)/shard_map/settle/pallas_call | solution.py:321

commit v4 on v3

--- a/solution.py
+++ b/solution.py
@@ -20,7 +20,7 @@
 
 def block_kernel(
     tokens, gain, w_qkv, gate, w_out, att_out, state_out,
-    tok, wts, qs, ks, vs, local, own, pay, got_c, got_x, got_y,
+    tok, wkv, wq, qs, ks, vs, local, own, pay, got_c, got_x, got_y,
     mine, mix, wown, wf, outs,
     in_sem, send_sem, recv_sem,
 ):
@@ -71,33 +71,60 @@
         return pl.ds(pl.multiple_of(owner * width, width), width)
 
     rows = [pl.ds(i * ROWS, ROWS) for i in range(n_chunks)]
-    tok_copies = [load(0, tokens.at[rows[0]], tok.at[rows[0]])]
-    w_copies = [load(n_chunks + j, w_qkv.at[j], wts.at[j]) for j in (1, 2, 0)]
-    tok_copies += [load(i, tokens.at[rows[i]], tok.at[rows[i]]) for i in range(1, n_chunks)]
-    own_copies = [
-        load(n_chunks + 3 + k, w_out.at[:, feature_block(plane(k))], wown.at[k]) for k in range(4)
-    ]
+    head_cols = [slice(h * HDIM, (h + 1) * HDIM) for h in range(heads)]
+
+    def load_tokens(i):
+        return load(i, tokens.at[rows[i]], tok.at[rows[i]])
+
+    def load_pair(h):
+        return [
+            load(n_chunks + 2 * h + j, w_qkv.at[1 + j, :, head_cols[h]], wkv.at[h, :, head_cols[j]])
+            for j in range(2)
+        ]
+
+    tok_copies = [load_tokens(0)]
+    pairs = [load_pair(0)]
+    tok_copies.append(load_tokens(1))
 
     g = gain[...].astype(F32).reshape(1, tok.shape[1])
 
     def normalize(i):
         tok_copies[i].wait()
+        if i + 2 < n_chunks:
+            tok_copies.append(load_tokens(i + 2))
         t = tok[rows[i], :].astype(F32)
         scale = lax.rsqrt(jnp.mean(t * t, axis=-1, keepdims=True) + 1e-05)
         tok[rows[i], :] = (t * scale * g).astype(BF16)
 
-    def project(i, j, dst):
-        out = jnp.dot(tok[rows[i], :], wts[j], preferred_element_type=F32)
-        dst[rows[i], :] = out.astype(BF16)
+    def project_pair(i, h):
+        out = jnp.dot(tok[rows[i], :], wkv[h], preferred_element_type=F32).astype(BF16)
+        ks[rows[i], head_cols[h]] = out[:, :HDIM]
+        vs[rows[i], head_cols[h]] = out[:, HDIM:]
+
+    def find_delta(h):
+        sig_k = elu_one(ks[:, head_cols[h]].astype(F32))
+        own[h, :HDIM] = lax.dot_general(
+            sig_k.astype(BF16), vs[:, head_cols[h]], (((0,), (0,)), ((), ())),
+            preferred_element_type=F32,
+        )
+        own[h, HDIM:] = jnp.broadcast_to(jnp.sum(sig_k, axis=0, keepdims=True), (16, HDIM))
+        pay[h, 0] = own[h].astype(BF16)
+        return remote(pay.at[h, 0], got_c.at[h], partner)
 
     normalize(0)
-    w_copies[0].wait()
-    w_copies[1].wait()
+    for copy in pairs[0]:
+        copy.wait()
     for i in range(n_chunks):
         if i + 1 < n_chunks:
             normalize(i + 1)
-        project(i, 1, ks)
-        project(i, 2, vs)
+        if i == 2:
+            pairs.append(load_pair(1))
+            q_copy = load(n_chunks + 4, w_qkv.at[0], wq)
+            own_copies = [
+                load(n_chunks + 5 + k, w_out.at[:, feature_block(plane(k))], wown.at[k])
+                for k in range(4)
+            ]
+        project_pair(i, 0)
         if i == 0:
             pl.semaphore_wait(barrier, len(peers))
             z_copies = []
@@ -111,22 +138,43 @@
                         w_out.at[slice_rows, feature_block(owner)],
                         wf.at[7 - k, 2 * c + q, x, y], zs[k - 1],
                     ))
-
-    norms = []
-    for h in range(heads):
-        cols = slice(h * HDIM, (h + 1) * HDIM)
-        sig_k = elu_one(ks[:, cols].astype(F32))
-        own[cols, :] = lax.dot_general(
-            sig_k.astype(BF16), vs[:, cols], (((0,), (0,)), ((), ())), preferred_element_type=F32
-        )
-        norms.append(jnp.sum(sig_k, axis=0, keepdims=True))
-    nrow = lax.broadcasted_iota(jnp.int32, (16, HDIM), 0)
-    tail = jnp.zeros((16, HDIM), F32)
-    for h in range(heads):
-        tail = jnp.where(nrow == h, norms[h], tail)
-    own[heads * HDIM :, :] = tail
-    pay[0] = own[...].astype(BF16)
-    swap = remote(pay.at[0], got_c, partner)
+    swaps = [find_delta(0)]
+    for copy in pairs[1]:
+        copy.wait()
+    for i in range(n_chunks):
+        project_pair(i, 1)
+
+    totals, befores, x_copies, y_copies = {}, {}, {}, {}
+
+    def send_x(h):
+        swaps[h].wait()
+        totals[h] = own[h] + got_c[h].astype(F32)
+        pay[h, 1] = totals[h].astype(BF16)
+        x_copies[h] = [remote(pay.at[h, 1], got_x.at[h, k - 1], xs[k - 1]) for k in (1, 2, 3)]
+
+    def send_y(h):
+        for copy in x_copies[h]:
+            copy.wait()
+        before = jnp.zeros_like(totals[h])
+        for k in (1, 2, 3):
+            before += jnp.where(x >= k, got_x[h, k - 1].astype(F32), 0.0)
+        befores[h] = before
+        pay[h, 2] = before.astype(BF16)
+        pay[h, 3] = (before + totals[h]).astype(BF16)
+        y_copies[h] = [
+            remote(pay.at[h, 2 + jnp.where(y + k < 4, 1, 0)], got_y.at[h, k - 1], ys[k - 1])
+            for k in (1, 2, 3)
+        ]
+
+    def finish_prefix(h):
+        for copy in y_copies[h]:
+            copy.wait()
+        prev = befores[h] + jnp.where(c == 1, got_c[h].astype(F32), 0.0)
+        for k in (1, 2, 3):
+            prev += got_y[h, k - 1].astype(F32)
+        state_out[0, h] = (prev[:HDIM] + own[h, :HDIM]) * (1.0 / seg)
+        norm_cols = jnp.transpose(jnp.broadcast_to(prev[HDIM : HDIM + 1], (HDIM, HDIM)))
+        return jnp.concatenate([prev[:HDIM], norm_cols], axis=1).astype(BF16)
 
     inv_sqrt = LOG2E / HDIM**0.5
     row_ids = lax.broadcasted_iota(jnp.int32, (ROWS, ROWS), 0)
@@ -149,31 +197,22 @@
         out = jnp.dot(w, vs[:end, cols], preferred_element_type=F32)
         local[rows[i], cols] = (1.0 - shares[h]) * out
 
-    work = [(h, i) for h in range(heads) for i in range(n_chunks)]
-    w_copies[2].wait()
-    for i in range(n_chunks):
-        project(i, 0, qs)
+    swaps.append(find_delta(1))
+    send_x(0)
+    q_copy.wait()
+    for i in range(n_chunks):
+        qs[rows[i], :] = jnp.dot(tok[rows[i], :], wq[...], preferred_element_type=F32).astype(BF16)
+    send_x(1)
     for copy in z_copies:
         copy.wait()
     one = [remote(wf.at[:, 2 * c, x, y], wf.at[:, 2 * c, x, y], peer) for peer in xs]
     one += [remote(wf.at[:, 2 * c + 1, x, y], wf.at[:, 2 * c + 1, x, y], peer) for peer in ys]
-    swap.wait()
-    total = own[...] + got_c[...].astype(F32)
-    pay[1] = total.astype(BF16)
-    x_copies = [remote(pay.at[1], got_x.at[k - 1], xs[k - 1]) for k in (1, 2, 3)]
-    for h, i in work[:4]:
-        attend(h, i)
-    for copy in x_copies:
-        copy.wait()
-    before = jnp.zeros_like(total)
-    for k in (1, 2, 3):
-        before += jnp.where(x >= k, got_x[k - 1].astype(F32), 0.0)
-    pay[2] = before.astype(BF16)
-    pay[3] = (before + total).astype(BF16)
-    y_copies = [
-        remote(pay.at[2 + jnp.where(y + k < 4, 1, 0)], got_y.at[k - 1], ys[k - 1])
-        for k in (1, 2, 3)
-    ]
+    for i in range(n_chunks):
+        attend(0, i)
+    send_y(0)
+    send_y(1)
+    for i in range(n_chunks - 1):
+        attend(1, i)
     for copy in one:
         copy.wait()
     two = [remote(wf.at[:, 2 * c, :, y], wf.at[:, 2 * c, :, y], peer) for peer in ys]
@@ -182,46 +221,37 @@
         remote(wf.at[:, 2 * c, :, y], wf.at[:, 2 * c, :, y], partner),
         remote(wf.at[:, 2 * c + 1, x], wf.at[:, 2 * c + 1, x], partner),
     ]
-    for h, i in work[4:]:
-        attend(h, i)
+    attend(1, n_chunks - 1)
     for i in range(n_chunks):
         qs[rows[i], :] = elu_one(qs[rows[i], :].astype(F32)).astype(BF16)
-    for copy in y_copies:
-        copy.wait()
-    prev = before + jnp.where(c == 1, got_c[...].astype(F32), 0.0)
-    for k in (1, 2, 3):
-        prev += got_y[k - 1].astype(F32)
-
-    memories = []
-    for h in range(heads):
-        cols = slice(h * HDIM, (h + 1) * HDIM)
-        state_out[0, h] = (prev[cols] + own[cols, :]) * (1.0 / seg)
-        norm = prev[heads * HDIM + h : heads * HDIM + h + 1]
-        norm_cols = jnp.transpose(jnp.broadcast_to(norm, (HDIM, HDIM)))
-        memories.append(jnp.concatenate([prev[cols], norm_cols], axis=1).astype(BF16))
+    memories = {}
 
     half = ROWS // 2
 
-    def blend(slot, quarter, t):
+    def blend(slot, quarter, t, h):
         block = pl.ds(pl.multiple_of(quarter * ROWS + t * half, half), half)
-        for h in range(heads):
-            cols = slice(h * HDIM, (h + 1) * HDIM)
-            both = jnp.dot(qs[block, cols], memories[h], preferred_element_type=F32)
-            got = shares[h] * both[:, :HDIM] / (1.0 + both[:, HDIM:])
-            mine[slot, t, :, cols] = (got + local[block, cols]).astype(BF16)
+        both = jnp.dot(qs[block, head_cols[h]], memories[h], preferred_element_type=F32)
+        got = shares[h] * both[:, :HDIM] / (1.0 + both[:, HDIM:])
+        mine[slot, t, h] = (got + local[block, head_cols[h]]).astype(BF16)
 
     towards = {1: plane(1), 2: plane(-2), 3: plane(3)}
     beside = (s, plane(-1))
     straight, next_door, handed = {}, {}, {}
     for t in range(2):
-        for k in (3, 2, 1):
-            blend(k, towards[k] // 2, t)
-            straight[t, k] = remote(mine.at[k, t], mix.at[k - 1, t], (s, towards[k]))
-        blend(0, pair, t)
-        next_door[t] = remote(mine.at[0, t], mix.at[3, t], beside)
+        for h in range(heads):
+            if t == 0:
+                memories[h] = finish_prefix(h)
+            for k in (3, 2, 1):
+                blend(k, towards[k] // 2, t, h)
+                straight[t, k, h] = remote(
+                    mine.at[k, t, h], mix.at[k - 1, t, h], (s, towards[k])
+                )
+            blend(0, pair, t, h)
+            next_door[t, h] = remote(mine.at[0, t, h], mix.at[3, t, h], beside)
     for t in range(2):
         for k in (1, 2, 3):
-            straight[t, k].wait()
+            for h in range(heads):
+                straight[t, k, h].wait()
             handed[t, k] = remote(mix.at[k - 1, t], mix.at[3 + k, t], beside)
         if t == 0:
             for k in (1, 2, 3):
@@ -239,17 +269,21 @@
     def place(off):
         return lax.rem(sign * off + 8, 8) - 1
 
+    def gathered(buffer, *at_slot):
+        return jnp.concatenate([buffer[(*at_slot, h)] for h in range(heads)], axis=1)
+
     def weight(off, k):
         return wf[place(off), k].reshape(width, width)
 
     last = []
     for t in range(2):
-        next_door[t].wait()
+        for h in range(heads):
+            next_door[t, h].wait()
         sums = []
         for k in range(4):
-            acc = jnp.dot(mine[0, t], wown[k], preferred_element_type=F32)
+            acc = jnp.dot(gathered(mine, 0, t), wown[k], preferred_element_type=F32)
             for slot, off in ((0, 1), (1, 2), (2, 3), (3, -1)):
-                acc += jnp.dot(mix[slot, t], weight(off, k), preferred_element_type=F32)
+                acc += jnp.dot(gathered(mix, slot, t), weight(off, k), preferred_element_type=F32)
             sums.append(acc)
         for k in (1, 2, 3):
             handed[t, k].wait()
@@ -257,7 +291,7 @@
         for k in (3, 2, 1, 0):
             acc = sums[k]
             for slot, off in ((4, -2), (5, -3), (6, -4)):
-                acc += jnp.dot(mix[slot, t], weight(off, k), preferred_element_type=F32)
+                acc += jnp.dot(gathered(mix, slot, t), weight(off, k), preferred_element_type=F32)
             if k == 0:
                 att_out[here, :] = acc.astype(BF16)
             else:
@@ -272,7 +306,7 @@
     width = w_qkv.shape[2]
     heads = width // HDIM
     n_chunks = seg // ROWS
-    pay = (heads * HDIM + 16, HDIM)
+    pay = (HDIM + 16, HDIM)
     vmem = pl.BlockSpec(memory_space=pltpu.VMEM)
     hbm = pl.BlockSpec(memory_space=pl.ANY)
     return pl.pallas_call(
@@ -285,24 +319,25 @@
         out_specs=(vmem, vmem),
         scratch_shapes=[
             pltpu.VMEM((seg, d), BF16),
-            pltpu.VMEM((3, d, width), BF16),
+            pltpu.VMEM((heads, d, 2 * HDIM), BF16),
+            pltpu.VMEM((d, width), BF16),
             pltpu.VMEM((seg, width), BF16),
             pltpu.VMEM((seg, width), BF16),
             pltpu.VMEM((seg, width), BF16),
             pltpu.VMEM((seg, width), F32),
-            pltpu.VMEM(pay, F32),
-            pltpu.VMEM((4,) + pay, BF16),
-            pltpu.VMEM(pay, BF16),
-            pltpu.VMEM((3,) + pay, BF16),
-            pltpu.VMEM((3,) + pay, BF16),
-            pltpu.VMEM((4, 2, ROWS // 2, width), BF16),
-            pltpu.VMEM((7, 2, ROWS // 2, width), BF16),
+            pltpu.VMEM((heads,) + pay, F32),
+            pltpu.VMEM((heads, 4) + pay, BF16),
+            pltpu.VMEM((heads,) + pay, BF16),
+            pltpu.VMEM((heads, 3) + pay, BF16),
+            pltpu.VMEM((heads, 3) + pay, BF16),
+            pltpu.VMEM((4, 2, heads, ROWS // 2, HDIM), BF16),
+            pltpu.VMEM((7, 2, heads, ROWS // 2, HDIM), BF16),
             pltpu.VMEM((4, width, width), BF16),
             pltpu.VMEM((7, 4, 4, 4, 16, width), BF16),
             pltpu.VMEM((3, 2, ROWS // 2, width), BF16),
-            pltpu.SemaphoreType.DMA((n_chunks + 7,)),
-            pltpu.SemaphoreType.DMA((64,)),
-            pltpu.SemaphoreType.DMA((64,)),
+            pltpu.SemaphoreType.DMA((n_chunks + 9,)),
+            pltpu.SemaphoreType.DMA((80,)),
+            pltpu.SemaphoreType.DMA((80,)),
         ],
         compiler_params=pltpu.CompilerParams(
             collective_id=0, has_side_effects=True, vmem_limit_bytes=60 << 20

time: 59.8 us -> 56.3 us (0.941)
  Pallas kernels: 58.2 us -> 55 us
    pallas_call x1, Pallas kernels: 56.3 us -> 53 us  [block(): pl.pallas_call(block_kernel, out_shape=(jax.ShapeDtypeStruct((seg, width)...]
where the time goes in v4:
time: 56.3 us; the launch traced here: 55.6 us
  Pallas kernels  55 us (98%)
  between operations  0.64 us (1%)
    pallas_call x1, Pallas kernels, block(): pl.pallas_call(block_kernel, out_shape=(jax.ShapeDtypeStruct((seg, width)...  53 us
    pallas_call x1, Pallas kernels, settle(): pl.pallas_call(settle_kernel, out_shape=tuple((jax.ShapeDtypeStruct(a.sha...  1.93 us

profile of v4, /device:TPU:32, one launch (start us, length us, event | category | flops | bytes accessed | tf_op | source)
XLA Modules:
  0.0 55.6 jit_solution(17445374413359438866)
XLA Ops:
  0.6 53.0 %block.1 = (bf16[1024,256]{1,0:T(8,128)(2,1)}, f32[1,2,128,128]{3,2,1,0:T(8,128)}) custom-call(bf16[1024,2048]{1,0:T(8,128)(2,1)} %tokens.1, bf16[2048]{0:T(1024)(128)(2,1)} %gain.1, bf16[3,2048,256]{2,1,0:T(8,128)(2,1)} %w_qkv.1, f32[2]{0:T(128)} %gate.1, bf16[256,2048]{1,0:T(8,128)(2,1)} %w_out.1), custom_call_target="tpu_custom_call" | custom-call | tf_op jit(solution)/shard_map/block/pallas_call | solution.py:312
  53.7 1.9 %settle.1 = (bf16[1024,256]{1,0:T(8,128)(2,1)}, f32[1,2,128,128]{3,2,1,0:T(8,128)}) custom-call(bf16[1024,256]{1,0:T(8,128)(2,1)} %get-tuple-element.4.att, f32[1,2,128,128]{3,2,1,0:T(8,128)} %get-tuple-element.5.state), custom_call_target="tpu_custom_call" | custom-call | tf_op jit(solution)/shard_map/settle/pallas_call | solution.py:356

commit v5 on v4

--- a/solution.py
+++ b/solution.py
@@ -19,8 +19,8 @@
 
 
 def block_kernel(
-    tokens, gain, w_qkv, gate, w_out, att_out, state_out,
-    tok, wkv, wq, qs, ks, vs, local, own, pay, got_c, got_x, got_y,
+    tokens, gain_in, w_qkv, gate_in, w_out, att_out, state_out,
+    gain, gate, tok, wkv, wq, qs, ks, vs, local, own, pay, got_c, got_x, got_y,
     mine, mix, wown, wf, outs,
     in_sem, send_sem, recv_sem,
 ):
@@ -82,10 +82,14 @@
             for j in range(2)
         ]
 
+    gain_copy = load(n_chunks + 9, gain_in, gain)
+    gate_copy = load(n_chunks + 10, gate_in, gate)
     tok_copies = [load_tokens(0)]
     pairs = [load_pair(0)]
     tok_copies.append(load_tokens(1))
 
+    gain_copy.wait()
+    gate_copy.wait()
     g = gain[...].astype(F32).reshape(1, tok.shape[1])
 
     def normalize(i):
@@ -315,9 +319,11 @@
             jax.ShapeDtypeStruct((seg, width), BF16),
             jax.ShapeDtypeStruct((1, heads, HDIM, HDIM), F32),
         ),
-        in_specs=[hbm, vmem, hbm, pl.BlockSpec(memory_space=pltpu.SMEM), hbm],
+        in_specs=[hbm] * 5,
         out_specs=(vmem, vmem),
         scratch_shapes=[
+            pltpu.VMEM((d,), BF16),
+            pltpu.SMEM((heads,), F32),
             pltpu.VMEM((seg, d), BF16),
             pltpu.VMEM((heads, d, 2 * HDIM), BF16),
             pltpu.VMEM((d, width), BF16),
@@ -335,12 +341,12 @@
             pltpu.VMEM((4, width, width), BF16),
             pltpu.VMEM((7, 4, 4, 4, 16, width), BF16),
             pltpu.VMEM((3, 2, ROWS // 2, width), BF16),
-            pltpu.SemaphoreType.DMA((n_chunks + 9,)),
+            pltpu.SemaphoreType.DMA((n_chunks + 11,)),
             pltpu.SemaphoreType.DMA((80,)),
             pltpu.SemaphoreType.DMA((80,)),
         ],
         compiler_params=pltpu.CompilerParams(
-            collective_id=0, has_side_effects=True, vmem_limit_bytes=60 << 20
+            collective_id=0, has_side_effects=True, vmem_limit_bytes=53 << 20
         ),
         name="block",
     )(tokens, gain, w_qkv, gate, w_out)
@@ -358,12 +364,14 @@
         out_shape=tuple(jax.ShapeDtypeStruct(a.shape, a.dtype) for a in arrays),
         in_specs=[vmem, vmem],
         out_specs=(vmem, vmem),
-        compiler_params=pltpu.CompilerParams(vmem_limit_bytes=60 << 20),
+        compiler_params=pltpu.CompilerParams(vmem_limit_bytes=8 << 20),
         name="settle",
     )(*arrays)
 
 
 def on_device(tokens, norm_gain, w_qkv, mem_gate, w_out):
+    norm_gain = pltpu.with_memory_space_constraint(norm_gain, pltpu.HBM)
+    mem_gate = pltpu.with_memory_space_constraint(mem_gate, pltpu.HBM)
     return settle(*block(tokens, norm_gain, w_qkv, mem_gate, w_out))
 
 

time: 56.3 us -> 53.6 us (0.952)
  Pallas kernels: 55 us -> 52.3 us
    pallas_call x1, Pallas kernels: 53 us -> 51.4 us  [block(): pl.pallas_call(block_kernel, out_shape=(jax.ShapeDtypeStruct((seg, width)...]
    pallas_call x1, Pallas kernels: 1.93 us -> 0.87 us  [settle(): pl.pallas_call(settle_kernel, out_shape=tuple((jax.ShapeDtypeStruct(a.sha...]
where the time goes in v5:
time: 53.6 us; the launch traced here: 52.9 us
  Pallas kernels  52.3 us (98%)
  between operations  0.64 us (1%)
    pallas_call x1, Pallas kernels, block(): pl.pallas_call(block_kernel, out_shape=(jax.ShapeDtypeStruct((seg, width)...  51.4 us

profile of v5, /device:TPU:32, one launch (start us, length us, event | category | flops | bytes accessed | tf_op | source)
XLA Modules:
  0.0 52.9 jit_solution(142582986362825492)
XLA Ops:
  0.6 51.4 %block.1 = (bf16[1024,256]{1,0:T(8,128)(2,1)S(1)}, f32[1,2,128,128]{3,2,1,0:T(8,128)S(1)}) custom-call(bf16[1024,2048]{1,0:T(8,128)(2,1)} %tokens.1, bf16[2048]{0:T(1024)(128)(2,1)} %gain_in.1, bf16[3,2048,256]{2,1,0:T(8,128)(2,1)} %w_qkv.1, f32[2]{0:T(128)} %gate_in.1, bf16[256,2048]{1,0:T(8,128)(2,1)} %w_out.1), custom_call_target="tpu_custom_call" | custom-call | tf_op jit(solution)/shard_map/block/pallas_call | solution.py:316
  52.0 0.9 %settle.1 = (bf16[1024,256]{1,0:T(8,128)(2,1)}, f32[1,2,128,128]{3,2,1,0:T(8,128)}) custom-call(bf16[1024,256]{1,0:T(8,128)(2,1)S(1)} %get-tuple-element.4.att, f32[1,2,128,128]{3,2,1,0:T(8,128)S(1)} %get-tuple-element.5.state), custom_call_target="tpu_custom_call" | custom-call | tf_op jit(solution)/shard_map/settle/pallas_call | solution.py:362

commit v6 on v5

--- a/solution.py
+++ b/solution.py
@@ -46,6 +46,7 @@
     zs = [(s, lax.rem(z + k, 8)) for k in range(1, 8)]
     peers = [partner] + xs + ys + zs
 
+    got_x[...] = jnp.zeros_like(got_x)
     barrier = pltpu.get_barrier_semaphore()
     for peer in peers:
         pl.semaphore_signal(barrier, inc=1, device_id=peer, device_id_type=MESH)
@@ -57,14 +58,17 @@
 
     used = [0]
 
-    def remote(src, dst, peer):
+    def remote(src, dst, peer, wanted=None):
         i = used[0]
         used[0] += 1
         copy = pltpu.make_async_remote_copy(
             src_ref=src, dst_ref=dst, send_sem=send_sem.at[i], recv_sem=recv_sem.at[i],
             device_id=peer, device_id_type=MESH,
         )
-        copy.start()
+        if wanted is None:
+            copy.start()
+        else:
+            pl.when(wanted)(copy.start)
         return copy
 
     def feature_block(owner):
@@ -154,11 +158,14 @@
         swaps[h].wait()
         totals[h] = own[h] + got_c[h].astype(F32)
         pay[h, 1] = totals[h].astype(BF16)
-        x_copies[h] = [remote(pay.at[h, 1], got_x.at[h, k - 1], xs[k - 1]) for k in (1, 2, 3)]
+        x_copies[h] = [
+            remote(pay.at[h, 1], got_x.at[h, k - 1], xs[k - 1], x + k < 4) for k in (1, 2, 3)
+        ]
 
     def send_y(h):
-        for copy in x_copies[h]:
-            copy.wait()
+        for k in (1, 2, 3):
+            pl.when(x + k < 4)(x_copies[h][k - 1].wait_send)
+            pl.when(x >= k)(x_copies[h][k - 1].wait_recv)
         before = jnp.zeros_like(totals[h])
         for k in (1, 2, 3):
             before += jnp.where(x >= k, got_x[h, k - 1].astype(F32), 0.0)
@@ -214,9 +221,10 @@
     for i in range(n_chunks):
         attend(0, i)
     send_y(0)
+    for i in range(n_chunks - 2):
+        attend(1, i)
     send_y(1)
-    for i in range(n_chunks - 1):
-        attend(1, i)
+    attend(1, n_chunks - 2)
     for copy in one:
         copy.wait()
     two = [remote(wf.at[:, 2 * c, :, y], wf.at[:, 2 * c, :, y], peer) for peer in ys]

time: 53.6 us -> 52.8 us (0.985)
  the two profiles are of different devices: /device:TPU:32 before, /device:TPU:6 now
where the time goes in v6:
time: 52.8 us; the launch traced here: 52.7 us
  Pallas kernels  52.1 us (99%)
  between operations  0.64 us (1%)
    pallas_call x1, Pallas kernels, block(): pl.pallas_call(block_kernel, out_shape=(jax.ShapeDtypeStruct((seg, width)...  51.2 us

profile of v6, /device:TPU:6, one launch (start us, length us, event | category | flops | bytes accessed | tf_op | source)
XLA Modules:
  0.0 52.7 jit_solution(8799305509352742593)
XLA Ops:
  0.6 51.2 %block.1 = (bf16[1024,256]{1,0:T(8,128)(2,1)S(1)}, f32[1,2,128,128]{3,2,1,0:T(8,128)S(1)}) custom-call(bf16[1024,2048]{1,0:T(8,128)(2,1)} %tokens.1, bf16[2048]{0:T(1024)(128)(2,1)} %gain_in.1, bf16[3,2048,256]{2,1,0:T(8,128)(2,1)} %w_qkv.1, f32[2]{0:T(128)} %gate_in.1, bf16[256,2048]{1,0:T(8,128)(2,1)} %w_out.1), custom_call_target="tpu_custom_call" | custom-call | tf_op jit(solution)/shard_map/block/pallas_call | solution.py:324
  51.9 0.9 %settle.1 = (bf16[1024,256]{1,0:T(8,128)(2,1)}, f32[1,2,128,128]{3,2,1,0:T(8,128)}) custom-call(bf16[1024,256]{1,0:T(8,128)(2,1)S(1)} %get-tuple-element.4.att, f32[1,2,128,128]{3,2,1,0:T(8,128)S(1)} %get-tuple-element.5.state), custom_call_target="tpu_custom_call" | custom-call | tf_op jit(solution)/shard_map/settle/pallas_call | solution.py:370
